TPU v7x, 32 devices: a whole 2x2x4 slice. The times are simulated.
32 devices in a mesh: grp: 2 (over x), seq: 16 (over z, y, core).
Axes of the slice: x: 2, y: 2, z: 4, core: 2. Of those that a mesh axis runs over, the one named last changes fastest.
Arguments:
- fresh_query: bfloat16 [4096, 4096], P(('grp', 'seq')), parts along dimension 0, may hold values from -80 to 80
- fresh_key: bfloat16 [4096, 4096], P(('grp', 'seq')), parts along dimension 0, may hold values from -4 to 4
- fresh_value: bfloat16 [4096, 4096], P(('grp', 'seq')), parts along dimension 0, may hold values from -4 to 4
- stale_key: bfloat16 [8192, 4096], P('grp', 'seq'), parts along dimension 0, may hold values from -4 to 4
- stale_value: bfloat16 [8192, 4096], P('grp', 'seq'), parts along dimension 0, may hold values from -4 to 4
- patch_start: int32 [2], P('grp'), parts along dimension 0, may hold values from 0 to 2048
- timestep: int32 [2], P('grp'), parts along dimension 0, may hold values from 0 to 34
- gate_table: float32 [35, 4096], replicated, may hold values from -4 to 4
Outputs:
- gated: bfloat16 [4096, 4096], P(('grp', 'seq')), parts along dimension 0
There are 2 independent parts, one for each index of `grp`. A program takes and returns all parts, laid end to end along the dimension named above; an argument that names none is the same for every part. Nothing has to cross between parts.
All inputs are finite; a program needn't handle non-finite values.
Results may differ from a plain program's by a relative error of at most 0.0056.
Values may be sent and summed in bfloat16 or wider, within the bound.
No kernel may reach another device: no remote copies, remote signals or barrier semaphores. Data moves between devices by JAX's collectives and lax.ppermute only.
A program may use at most 64 MiB of HBM per device.

v0:
```python
import jax
import jax.numpy as jnp
from jax import lax
from jax.sharding import PartitionSpec as P

HD = 128


def attend_group(queries, keys, values):
    scores = jnp.dot(queries, keys.T, preferred_element_type=jnp.float32) * HD ** (-0.5)
    row_max = jnp.max(scores, axis=1)
    expo = jnp.exp(scores - row_max[:, None])
    total = jnp.sum(expo, axis=1)
    output = jnp.dot(expo.astype(jnp.bfloat16), values, preferred_element_type=jnp.float32)
    return (row_max, total, output)


def attend_blocks(queries, keys, values):
    all_rows = queries.shape[0]
    block_rows = min(512, all_rows)
    blocks = queries.reshape(all_rows // block_rows, block_rows, queries.shape[1])
    row_max, total, output = lax.map(lambda q_block: attend_group(q_block, keys, values), blocks)
    return (
        row_max.reshape(all_rows),
        total.reshape(all_rows),
        output.reshape(all_rows, values.shape[1]),
    )


def old_partials(queries_all, old_key, old_value, heads_dev):
    results = []
    for head_idx in range(heads_dev):
        cols = slice(head_idx * HD, (head_idx + 1) * HD)
        results.append(
            attend_blocks(queries_all[:, head_idx, :], old_key[:, cols], old_value[:, cols])
        )
    return results


def shards(
    fresh_query, fresh_key, fresh_value, stale_key, stale_value, patch_start, timestep, gate_table
):
    tok_rows = fresh_query.shape[0]
    model_width = fresh_query.shape[1]
    heads_dev = stale_key.shape[1] // HD
    patch_rows = tok_rows * lax.axis_size("seq")
    seq_rows = stale_key.shape[0]
    query_heads = fresh_query.reshape(tok_rows, model_width // HD, HD)
    key_heads = fresh_key.reshape(tok_rows, model_width // HD, HD)
    value_heads = fresh_value.reshape(tok_rows, model_width // HD, HD)
    shift_by = -(patch_start[0] + patch_rows)
    old_key = jnp.roll(stale_key, shift_by, axis=0)[: seq_rows - patch_rows]
    old_value = jnp.roll(stale_value, shift_by, axis=0)[: seq_rows - patch_rows]
    queries_all, keys_all, values_all = (
        lax.all_to_all(query_heads, "seq", split_axis=1, concat_axis=0, tiled=True),
        lax.all_to_all(key_heads, "seq", split_axis=1, concat_axis=0, tiled=True),
        lax.all_to_all(value_heads, "seq", split_axis=1, concat_axis=0, tiled=True),
    )
    old_parts = old_partials(queries_all, old_key, old_value, heads_dev)
    outputs = []
    for head_idx in range(heads_dev):
        max_old, sum_old, out_old = old_parts[head_idx]
        max_new, sum_new, out_new = attend_blocks(
            queries_all[:, head_idx, :], keys_all[:, head_idx, :], values_all[:, head_idx, :]
        )
        top = jnp.maximum(max_old, max_new)
        scale_old = jnp.exp(max_old - top)
        scale_new = jnp.exp(max_new - top)
        numer = scale_old[:, None] * out_old + scale_new[:, None] * out_new
        denom = scale_old * sum_old + scale_new * sum_new
        outputs.append((numer / denom[:, None]).astype(jnp.bfloat16))
    heads_out = jnp.stack(outputs, axis=1)
    back_home = lax.all_to_all(heads_out, "seq", split_axis=0, concat_axis=1, tiled=True)
    attn = back_home.reshape(tok_rows, model_width)
    gate_row = lax.dynamic_slice_in_dim(gate_table, timestep[0], 1, 0)
    return (attn.astype(jnp.float32) * gate_row).astype(jnp.bfloat16)


def solution(mesh):
    return jax.shard_map(
        shards,
        mesh=mesh,
        in_specs=(
            P(("grp", "seq"), None),
            P(("grp", "seq"), None),
            P(("grp", "seq"), None),
            P("grp", "seq"),
            P("grp", "seq"),
            P("grp"),
            P("grp"),
            P(),
        ),
        out_specs=P(("grp", "seq"), None),
        check_vma=False,
    )
```

profile of v0, /device:TPU:11, one launch (start us, length us, event | category | flops | bytes accessed | tf_op | source)
XLA Modules:
  0.0 210.6 jit_solution(3825884178690398125)
XLA Ops:
  0.0 1.7 copy.40
  1.8 1.3 copy.41
  3.1 6.6 %all-to-all-start = ((bf16[128,32,128]{2,0,1:T(8,128)(2,1)}), bf16[128,32,128]{2,0,1:T(8,128)(2,1)S(1)}, u32[]{:S(2)}, u32[]{:S(2)}) async-start(bf16[128,32,128]{2,0,1:T(8,128)(2,1)} %copy.41), calls=%async_computation | async-start | bytes 2097152 | tf_op jit(solution)/shard_map/all_to_all | solution.py:55
  10.3 1.3 copy.43
  11.6 2.3 %copy.46 = bf16[128,4096]{0,1:T(8,128)(2,1)} copy(bf16[128,4096]{1,0:T(8,128)(2,1)} %param.20) | data formatting | bytes 2097152 | tf_op args[2]
  13.9 20.7 %all-to-all-done = bf16[128,32,128]{2,0,1:T(8,128)(2,1)S(1)} async-done(((bf16[128,32,128]{2,0,1:T(8,128)(2,1)}), bf16[128,32,128]{2,0,1:T(8,128)(2,1)S(1)}, u32[]{:S(2)}, u32[]{:S(2)}) %all-to-all-start) | async-done | bytes 1048608 | tf_op jit(solution)/shard_map/all_to_all | solution.py:55
  34.6 4.8 %all-to-all-start.1 = ((bf16[128,32,128]{0,2,1:T(8,128)(2,1)}), bf16[128,32,128]{0,2,1:T(8,128)(2,1)}, u32[]{:S(2)}, u32[]{:S(2)}) async-start(bf16[128,32,128]{0,2,1:T(8,128)(2,1)} %bitcast.22), calls=%async_computation.1 | async-start | bytes 2097152 | tf_op jit(solution)/shard_map/all_to_all | solution.py:56
  39.3 4.8 %fusion.68 = (bf16[4096,256]{1,0:T(8,128)(2,1)S(1)}, bf16[4096,256]{1,0:T(8,128)(2,1)S(1)}) fusion(s32[]{:T(128)S(6)} %select_n.17, bf16[4096,256]{1,0:T(8,128)(2,1)} %param.22, bf16[4096,256]{1,0:T(8,128)(2,1)} %param.21), kind=kLoop, calls=%fused_computation.60 | loop fusion | flops 8388608 | bytes 8388612 | tf_op jit(solution)/shard_map/jit(_roll_dynamic)/concatenate | solution.py:53
  44.4 1.1 copy-done.3
  45.5 0.9 fusion.81
  46.4 17.9 %all-to-all-done.1 = bf16[128,32,128]{0,2,1:T(8,128)(2,1)} async-done(((bf16[128,32,128]{0,2,1:T(8,128)(2,1)}), bf16[128,32,128]{0,2,1:T(8,128)(2,1)}, u32[]{:S(2)}, u32[]{:S(2)}) %all-to-all-start.1) | async-done | bytes 1048608 | tf_op jit(solution)/shard_map/all_to_all | solution.py:56
  64.4 4.8 %all-to-all-start.2 = ((bf16[128,32,128]{0,2,1:T(8,128)(2,1)}), bf16[128,32,128]{0,2,1:T(8,128)(2,1)}, u32[]{:S(2)}, u32[]{:S(2)}) async-start(bf16[128,32,128]{0,2,1:T(8,128)(2,1)} %bitcast.163), calls=%async_computation.2 | async-start | bytes 2097152 | tf_op jit(solution)/shard_map/all_to_all | solution.py:57
  69.1 1.0 broadcast.120.clone.3
  70.2 13.2 %while.56 = (s32[]{:T(128)}, f32[4,512]{1,0:T(4,128)S(1)}, f32[4,512]{1,0:T(4,128)S(1)}, f32[4,512,128]{2,1,0:T(8,128)}, bf16[4,512,128]{2,1,0:T(8,128)(2,1)S(1)...) while((s32[]{:T(128)}, f32[4,512]{1,0:T(4,128)S(1)}, ...), condition=%wide.region_3.5_spmd, body=%wide.region_0.4_spmd.sunk | while | flops 545258496 | bytes 14041705 | solution.py:22
  71.0 1.6 fusion.114
  74.2 1.6 fusion.114
  77.5 1.6 fusion.114
  80.8 1.6 fusion.114
  83.4 2.4 %copy.45 = bf16[16,128,2,128]{3,1,0,2:T(8,128)(2,1)} copy(bf16[16,128,2,128]{1,3,2,0:T(8,128)(2,1)} %bitcast.25) | data formatting | bytes 2097152 | tf_op jit(solution)/shard_map/all_to_all | solution.py:56
  85.8 8.3 %all-to-all-done.2 = bf16[128,32,128]{0,2,1:T(8,128)(2,1)} async-done(((bf16[128,32,128]{0,2,1:T(8,128)(2,1)}), bf16[128,32,128]{0,2,1:T(8,128)(2,1)}, u32[]{:S(2)}, u32[]{:S(2)}) %all-to-all-start.2) | async-done | bytes 1048608 | tf_op jit(solution)/shard_map/all_to_all | solution.py:57
  94.1 2.3 %copy.48 = bf16[16,128,2,128]{3,1,0,2:T(8,128)(2,1)} copy(bf16[16,128,2,128]{1,3,2,0:T(8,128)(2,1)} %bitcast.31) | data formatting | bytes 2097152 | tf_op jit(solution)/shard_map/all_to_all | solution.py:57
  96.4 2.5 %slice_bitcast_fusion.2 = (bf16[2048,128]{1,0:T(8,128)(2,1)S(1)}, bf16[2048,128]{1,0:T(8,128)(2,1)S(1)}, bf16[2048,128]{1,0:T(8,128)(2,1)S(1)}, bf16[2048,128]{1,0:T(8,128)(2,1)}) fusion(bf16[2048,2,128]{2,0,1:T(8,128)(2,1)} %bitcast.168, bf16[2048,2,128]{2,0,1:T(8,128)(2,1)} %bitcast.167), kind=kLoop, calls=%fused_computation.70 | loop fusion | bytes 4194304 | tf_op jit(solution)/shard_map/squeeze | solution.py:64
  98.9 1.0 broadcast.120.clone.2
  99.9 17.5 %while.57 = (s32[]{:T(128)}, f32[4,512]{1,0:T(4,128)S(1)}, f32[4,512]{1,0:T(4,128)S(1)}, f32[4,512,128]{2,1,0:T(8,128)}, bf16[4,512,128]{2,1,0:T(8,128)(2,1)}, /...) while((s32[]{:T(128)}, f32[4,512]{1,0:T(4,128)S(1)}, ...), condition=%wide.region_7.9_spmd, body=%wide.region_4.8_spmd.sunk | while | flops 545258496 | bytes 14042213 | solution.py:22
  99.9 1.9 multiply_reduce_fusion.9
  101.8 1.5 fusion.119
  104.3 1.9 multiply_reduce_fusion.9
  106.2 1.6 fusion.119
  108.7 1.9 multiply_reduce_fusion.9
  110.6 1.5 fusion.119
  113.1 1.9 multiply_reduce_fusion.9
  115.0 1.6 fusion.119
  117.5 1.0 broadcast.120.clone.1
  118.6 16.7 %while.58 = (s32[]{:T(128)}, f32[4,512]{1,0:T(4,128)S(1)}, f32[4,512]{1,0:T(4,128)S(1)}, f32[4,512,128]{2,1,0:T(8,128)}, bf16[4,512,128]{2,1,0:T(8,128)(2,1)}, /...) while((s32[]{:T(128)}, f32[4,512]{1,0:T(4,128)S(1)}, ...), condition=%wide.region_11.13_spmd, body=%wide.region_8.12_spmd.sunk | while | flops 545258496 | bytes 14042213 | solution.py:22
  118.6 1.7 multiply_reduce_fusion.10
  120.2 1.6 fusion.124
  122.7 1.7 multiply_reduce_fusion.10
  124.4 1.6 fusion.124
  126.9 1.7 multiply_reduce_fusion.10
  128.6 1.6 fusion.124
  131.1 1.7 multiply_reduce_fusion.10
  132.8 1.6 fusion.124
  135.4 13.9 %while.59 = (s32[]{:T(128)}, f32[4,512]{1,0:T(4,128)S(1)}, f32[4,512]{1,0:T(4,128)S(1)}, f32[4,512,128]{2,1,0:T(8,128)S(1)}, bf16[4,512,128]{2,1,0:T(8,128)(2,1)...) while((s32[]{:T(128)}, f32[4,512]{1,0:T(4,128)S(1)}, ...), condition=%wide.region_15.17_spmd, body=%wide.region_12.16_spmd.sunk | while | flops 545258496 | bytes 14041705 | solution.py:22
  135.4 1.7 multiply_reduce_fusion.11
  137.1 0.8 fusion.129
  138.0 0.8 fusion.128
  138.9 1.7 multiply_reduce_fusion.11
  140.6 0.9 fusion.129
  141.4 0.8 fusion.128
  142.4 1.7 multiply_reduce_fusion.11
  144.1 0.9 fusion.129
  144.9 0.8 fusion.128
  145.9 1.7 multiply_reduce_fusion.11
  147.6 0.9 fusion.129
  148.4 0.8 fusion.128
  149.4 10.3 %divide_convert_fusion.1 = bf16[2048,1,128]{2,1,0:T(2,128)(2,1)S(1)} fusion(f32[2048,1,128]{2,1,0:T(1,128)} %bitcast.35, f32[2048,1,128]{2,1,0:T(1,128)} %bitcast.34, f32[2048]{0:T(1024)S(1)} %get-tuple-element.230, f32[2048]{0:T(1024)S(1)} %get-tuple-element.232, f32[2048]{0:T(1024)S(1)} %get-tuple-element.231), kind=kLoop, calls=%fused_computation.67 | loop fusion | flops 1310720 | bytes 2646016 | tf_op jit(solution)/shard_map/convert_element_type | solution.py:71
  159.7 10.2 %divide_convert_fusion = bf16[2048,1,128]{2,1,0:T(2,128)(2,1)S(1)} fusion(f32[2048,1,128]{2,1,0:T(1,128)S(1)} %bitcast.161, f32[2048,1,128]{2,1,0:T(1,128)} %bitcast.39, f32[2048]{0:T(1024)S(1)} %get-tuple-element.233, f32[2048]{0:T(1024)S(1)} %get-tuple-element.235, f32[2048]{0:T(1024)S(1)} %get-tuple-element.234), kind=kLoop, calls=%fused_computation.66 | loop fusion | flops 1310720 | bytes 2646016 | tf_op jit(solution)/shard_map/convert_element_type | solution.py:71
  170.0 3.4 %pad_maximum_fusion = bf16[2048,2,128]{2,1,0:T(2,128)(2,1)} fusion(bf16[2048,1,128]{2,1,0:T(2,128)(2,1)S(1)} %divide_convert_fusion, bf16[2048,1,128]{2,1,0:T(2,128)(2,1)S(1)} %divide_convert_fusion.1), kind=kLoop, calls=%fused_computation.65 | loop fusion | flops 2097152 | bytes 2097152 | tf_op jit(solution)/shard_map/stack | solution.py:72
  173.4 4.8 %all-to-all-start.3 = ((bf16[2048,2,128]{2,1,0:T(2,128)(2,1)}), bf16[2048,2,128]{2,1,0:T(2,128)(2,1)S(1)}, u32[]{:S(2)}, u32[]{:S(2)}) async-start(bf16[2048,2,128]{2,1,0:T(2,128)(2,1)} %pad_maximum_fusion), calls=%async_computation.3 | async-start | bytes 2097152 | tf_op jit(solution)/shard_map/all_to_all | solution.py:73
  178.9 24.2 %all-to-all-done.3 = bf16[2048,2,128]{2,1,0:T(2,128)(2,1)S(1)} async-done(((bf16[2048,2,128]{2,1,0:T(2,128)(2,1)}), bf16[2048,2,128]{2,1,0:T(2,128)(2,1)S(1)}, u32[]{:S(2)}, u32[]{:S(2)}) %all-to-all-start.3) | async-done | bytes 1048608 | tf_op jit(solution)/shard_map/all_to_all | solution.py:73
  203.2 1.6 convert_bitcast_fusion
  204.8 1.9 copy.50
  206.7 1.6 fusion.70
  208.4 2.3 %copy.51 = bf16[128,4096]{1,0:T(8,128)(2,1)} copy(bf16[128,4096]{0,1:T(8,128)(2,1)} %fusion.70) | data formatting | bytes 2097152 | tf_op jit(solution)/shard_map/convert_element_type | solution.py:76
  (81 shorter events, 15.0 us)
Async XLA Ops:
  0.0 178.8 %copy-start = (f32[35,4096]{1,0:T(8,128)S(1)}, f32[35,4096]{1,0:T(8,128)}, u32[]{:S(2)}) copy-start(f32[35,4096]{1,0:T(8,128)} %param.25) | copy-start | bytes 1720324
  0.0 10.3 %copy-start.4 = (bf16[128,4096]{1,0:T(8,128)(2,1)S(1)}, bf16[128,4096]{1,0:T(8,128)(2,1)}, u32[]{:S(2)}) copy-start(bf16[128,4096]{1,0:T(8,128)(2,1)} %param.19) | copy-start | bytes 3145732
  3.1 31.5 %all-to-all-start = ((bf16[128,32,128]{2,0,1:T(8,128)(2,1)}), bf16[128,32,128]{2,0,1:T(8,128)(2,1)S(1)}, u32[]{:S(2)}, u32[]{:S(2)}) async-start(bf16[128,32,128]{2,0,1:T(8,128)(2,1)} %copy.41), calls=%async_computation | async-start | bytes 2097152 | tf_op jit(solution)/shard_map/all_to_all | solution.py:55
  34.6 9.6 %copy-start.2 = (bf16[128,32,128]{2,0,1:T(8,128)(2,1)}, bf16[128,32,128]{2,0,1:T(8,128)(2,1)S(1)}, u32[]{:S(2)}) copy-start(bf16[128,32,128]{2,0,1:T(8,128)(2,1)S(1)} %all-to-all-done) | copy-start | bytes 3145732
  34.6 29.8 %all-to-all-start.1 = ((bf16[128,32,128]{0,2,1:T(8,128)(2,1)}), bf16[128,32,128]{0,2,1:T(8,128)(2,1)}, u32[]{:S(2)}, u32[]{:S(2)}) async-start(bf16[128,32,128]{0,2,1:T(8,128)(2,1)} %bitcast.22), calls=%async_computation.1 | async-start | bytes 2097152 | tf_op jit(solution)/shard_map/all_to_all | solution.py:56
  44.2 1.2 copy-start.3
  64.4 29.8 %all-to-all-start.2 = ((bf16[128,32,128]{0,2,1:T(8,128)(2,1)}), bf16[128,32,128]{0,2,1:T(8,128)(2,1)}, u32[]{:S(2)}, u32[]{:S(2)}) async-start(bf16[128,32,128]{0,2,1:T(8,128)(2,1)} %bitcast.163), calls=%async_computation.2 | async-start | bytes 2097152 | tf_op jit(solution)/shard_map/all_to_all | solution.py:57
  83.3 13.1 %copy-start.1 = (bf16[4,512,128]{2,1,0:T(8,128)(2,1)}, bf16[4,512,128]{2,1,0:T(8,128)(2,1)S(1)}, u32[]{:S(2)}) copy-start(bf16[4,512,128]{2,1,0:T(8,128)(2,1)S(1)} %get-tuple-element.555) | copy-start | bytes 1572868
  173.4 29.7 %all-to-all-start.3 = ((bf16[2048,2,128]{2,1,0:T(2,128)(2,1)}), bf16[2048,2,128]{2,1,0:T(2,128)(2,1)S(1)}, u32[]{:S(2)}, u32[]{:S(2)}) async-start(bf16[2048,2,128]{2,1,0:T(2,128)(2,1)} %pad_maximum_fusion), calls=%async_computation.3 | async-start | bytes 2097152 | tf_op jit(solution)/shard_map/all_to_all | solution.py:73
where the time goes:
time: 212 us; the launch traced here: 211 us
  waiting for transfers between devices  71.2 us (34%)
  matrix products  46.4 us (22%)
  other arithmetic  45.1 us (21%)
  local copies, waits for them, and re-layouts  25.2 us (12%)
  starting transfers between devices  20.9 us (10%)
    dot_general x16, matrix products, attend_group(): jnp.dot(queries, keys.T, preferred_element_type=jnp.float32) * HD ** (-0.5)  24.3 us
    all_to_all x1, waiting for transfers between devices, shards(): lax.all_to_all(heads_out, 'seq', split_axis=0, concat_axis=1, tiled=True)  24.2 us
    dot_general x16, matrix products, attend_group(): jnp.dot(expo.astype(jnp.bfloat16), values, preferred_element_type=jnp.flo...  22.1 us
    all_to_all x1, waiting for transfers between devices, shards(): lax.all_to_all(query_heads, 'seq', split_axis=1, concat_axis=0, tiled=True)  20.7 us
    convert_element_type x2, other arithmetic, shards(): outputs.append((numer / denom[:, None]).astype(jnp.bfloat16))  20.5 us
    all_to_all x1, waiting for transfers between devices, shards(): lax.all_to_all(key_heads, 'seq', split_axis=1, concat_axis=0, tiled=True)  17.9 us
    reduce_sum x16, other arithmetic, attend_group(): total = jnp.sum(expo, axis=1)  13 us
    all_to_all x1, waiting for transfers between devices, shards(): lax.all_to_all(value_heads, 'seq', split_axis=1, concat_axis=0, tiled=True)  8.33 us
  transfers between devices with their start and end apart: 4, of which 4 were waited for; matrix products, arithmetic and copies ran while one was open for 12% of the time, Pallas kernels for 0%

commit v1 on v0

--- a/solution.py
+++ b/solution.py
@@ -70,7 +70,10 @@
         denom = scale_old * sum_old + scale_new * sum_new
         outputs.append((numer / denom[:, None]).astype(jnp.bfloat16))
     heads_out = jnp.stack(outputs, axis=1)
-    back_home = lax.all_to_all(heads_out, "seq", split_axis=0, concat_axis=1, tiled=True)
+    back_home = jnp.concatenate(
+        lax.all_to_all(jnp.stack(jnp.split(heads_out, lax.axis_size("seq"), axis=0)), "seq", 0, 0),
+        axis=1,
+    )
     attn = back_home.reshape(tok_rows, model_width)
     gate_row = lax.dynamic_slice_in_dim(gate_table, timestep[0], 1, 0)
     return (attn.astype(jnp.float32) * gate_row).astype(jnp.bfloat16)

time: 212 us -> 216 us (1.019)
  other arithmetic: 45.1 us -> 51.9 us
  local copies, waits for them, and re-layouts: 25.2 us -> 23 us
    unnamed x0 -> x15, other arithmetic: none -> 11.7 us
    convert_element_type x2 -> x1, local copies, waits for them, and re-layouts: 4.19 us -> 1.31 us  [shards(): return (attn.astype(jnp.float32) * gate_row).astype(jnp.bfloat16)]
    another operation x1, other arithmetic: 3.43 us -> 0.78 us  [shards(): jnp.stack(jnp.split(heads_out, lax.axis_size('seq'), axis=0))]
    convert_element_type x2 -> x1, other arithmetic: 3.21 us -> 0.71 us  [shards(): return (attn.astype(jnp.float32) * gate_row).astype(jnp.bfloat16)]
where the time goes in v1:
time: 216 us; the launch traced here: 215 us
  waiting for transfers between devices  71.2 us (33%)
  other arithmetic  51.9 us (24%)
  matrix products  46.4 us (21%)
  local copies, waits for them, and re-layouts  23 us (11%)
  starting transfers between devices  20.9 us (10%)
    dot_general x16, matrix products, attend_group(): jnp.dot(queries, keys.T, preferred_element_type=jnp.float32) * HD ** (-0.5)  24.3 us
    all_to_all x1, waiting for transfers between devices, shards(): lax.all_to_all(jnp.stack(jnp.split(heads_out, lax.axis_size('seq'), axis=...  24.2 us
    dot_general x16, matrix products, attend_group(): jnp.dot(expo.astype(jnp.bfloat16), values, preferred_element_type=jnp.flo...  22.1 us
    convert_element_type x2, other arithmetic, shards(): outputs.append((numer / denom[:, None]).astype(jnp.bfloat16))  20.8 us
    all_to_all x1, waiting for transfers between devices, shards(): lax.all_to_all(query_heads, 'seq', split_axis=1, concat_axis=0, tiled=True)  20.7 us
    all_to_all x1, waiting for transfers between devices, shards(): lax.all_to_all(key_heads, 'seq', split_axis=1, concat_axis=0, tiled=True)  17.9 us
    reduce_sum x16, other arithmetic, attend_group(): total = jnp.sum(expo, axis=1)  13 us
    unnamed x15, other arithmetic  11.7 us
  transfers between devices with their start and end apart: 4, of which 4 were waited for; matrix products, arithmetic and copies ran while one was open for 12% of the time, Pallas kernels for 0%

profile of v1, /device:TPU:11, one launch (start us, length us, event | category | flops | bytes accessed | tf_op | source)
XLA Modules:
  0.0 215.3 jit_solution(14512086072215667148)
XLA Ops:
  0.0 1.7 copy.91
  1.8 1.3 copy.92
  3.1 6.6 %all-to-all-start = ((bf16[128,32,128]{2,0,1:T(8,128)(2,1)}), bf16[128,32,128]{2,0,1:T(8,128)(2,1)S(1)}, u32[]{:S(2)}, u32[]{:S(2)}) async-start(bf16[128,32,128]{2,0,1:T(8,128)(2,1)} %copy.92), calls=%async_computation | async-start | bytes 2097152 | tf_op jit(solution)/shard_map/all_to_all | solution.py:55
  10.3 1.3 copy.94
  11.6 2.3 %copy.97 = bf16[128,4096]{0,1:T(8,128)(2,1)} copy(bf16[128,4096]{1,0:T(8,128)(2,1)} %param.20) | data formatting | bytes 2097152 | tf_op args[2]
  13.9 20.7 %all-to-all-done = bf16[128,32,128]{2,0,1:T(8,128)(2,1)S(1)} async-done(((bf16[128,32,128]{2,0,1:T(8,128)(2,1)}), bf16[128,32,128]{2,0,1:T(8,128)(2,1)S(1)}, u32[]{:S(2)}, u32[]{:S(2)}) %all-to-all-start) | async-done | bytes 1048608 | tf_op jit(solution)/shard_map/all_to_all | solution.py:55
  34.6 4.8 %all-to-all-start.1 = ((bf16[128,32,128]{0,2,1:T(8,128)(2,1)}), bf16[128,32,128]{0,2,1:T(8,128)(2,1)}, u32[]{:S(2)}, u32[]{:S(2)}) async-start(bf16[128,32,128]{0,2,1:T(8,128)(2,1)} %bitcast.22), calls=%async_computation.1 | async-start | bytes 2097152 | tf_op jit(solution)/shard_map/all_to_all | solution.py:56
  39.3 4.8 %fusion.68 = (bf16[4096,256]{1,0:T(8,128)(2,1)S(1)}, bf16[4096,256]{1,0:T(8,128)(2,1)S(1)}) fusion(s32[]{:T(128)S(6)} %select_n.17, bf16[4096,256]{1,0:T(8,128)(2,1)} %param.22, bf16[4096,256]{1,0:T(8,128)(2,1)} %param.21), kind=kLoop, calls=%fused_computation.60 | loop fusion | flops 8388608 | bytes 8388612 | tf_op jit(solution)/shard_map/jit(_roll_dynamic)/concatenate | solution.py:53
  44.4 1.1 copy-done.3
  45.5 0.9 fusion.98
  46.4 17.9 %all-to-all-done.1 = bf16[128,32,128]{0,2,1:T(8,128)(2,1)} async-done(((bf16[128,32,128]{0,2,1:T(8,128)(2,1)}), bf16[128,32,128]{0,2,1:T(8,128)(2,1)}, u32[]{:S(2)}, u32[]{:S(2)}) %all-to-all-start.1) | async-done | bytes 1048608 | tf_op jit(solution)/shard_map/all_to_all | solution.py:56
  64.4 4.8 %all-to-all-start.2 = ((bf16[128,32,128]{0,2,1:T(8,128)(2,1)}), bf16[128,32,128]{0,2,1:T(8,128)(2,1)}, u32[]{:S(2)}, u32[]{:S(2)}) async-start(bf16[128,32,128]{0,2,1:T(8,128)(2,1)} %bitcast.224), calls=%async_computation.2 | async-start | bytes 2097152 | tf_op jit(solution)/shard_map/all_to_all | solution.py:57
  69.1 1.0 broadcast.120.clone.3
  70.2 13.2 %while.56 = (s32[]{:T(128)}, f32[4,512]{1,0:T(4,128)S(1)}, f32[4,512]{1,0:T(4,128)S(1)}, f32[4,512,128]{2,1,0:T(8,128)}, bf16[4,512,128]{2,1,0:T(8,128)(2,1)S(1)...) while((s32[]{:T(128)}, f32[4,512]{1,0:T(4,128)S(1)}, ...), condition=%wide.region_3.5_spmd, body=%wide.region_0.4_spmd.sunk | while | flops 545258496 | bytes 14041705 | solution.py:22
  71.0 1.6 fusion.131
  72.5 0.8 fusion.130
  74.2 1.6 fusion.131
  75.8 0.8 fusion.130
  77.5 1.6 fusion.131
  79.1 0.8 fusion.130
  80.8 1.6 fusion.131
  83.4 2.4 %copy.96 = bf16[16,128,2,128]{3,1,0,2:T(8,128)(2,1)} copy(bf16[16,128,2,128]{1,3,2,0:T(8,128)(2,1)} %bitcast.25) | data formatting | bytes 2097152 | tf_op jit(solution)/shard_map/all_to_all | solution.py:56
  85.8 8.3 %all-to-all-done.2 = bf16[128,32,128]{0,2,1:T(8,128)(2,1)} async-done(((bf16[128,32,128]{0,2,1:T(8,128)(2,1)}), bf16[128,32,128]{0,2,1:T(8,128)(2,1)}, u32[]{:S(2)}, u32[]{:S(2)}) %all-to-all-start.2) | async-done | bytes 1048608 | tf_op jit(solution)/shard_map/all_to_all | solution.py:57
  94.1 2.3 %copy.99 = bf16[16,128,2,128]{3,1,0,2:T(8,128)(2,1)} copy(bf16[16,128,2,128]{1,3,2,0:T(8,128)(2,1)} %bitcast.31) | data formatting | bytes 2097152 | tf_op jit(solution)/shard_map/all_to_all | solution.py:57
  96.4 2.5 %slice_bitcast_fusion.2 = (bf16[2048,128]{1,0:T(8,128)(2,1)S(1)}, bf16[2048,128]{1,0:T(8,128)(2,1)S(1)}, bf16[2048,128]{1,0:T(8,128)(2,1)S(1)}, bf16[2048,128]{1,0:T(8,128)(2,1)}) fusion(bf16[2048,2,128]{2,0,1:T(8,128)(2,1)} %bitcast.229, bf16[2048,2,128]{2,0,1:T(8,128)(2,1)} %bitcast.228), kind=kLoop, calls=%fused_computation.68 | loop fusion | bytes 4194304 | tf_op jit(solution)/shard_map/squeeze | solution.py:64
  98.9 1.0 broadcast.120.clone.2
  99.9 17.5 %while.57 = (s32[]{:T(128)}, f32[4,512]{1,0:T(4,128)S(1)}, f32[4,512]{1,0:T(4,128)S(1)}, f32[4,512,128]{2,1,0:T(8,128)}, bf16[4,512,128]{2,1,0:T(8,128)(2,1)}, /...) while((s32[]{:T(128)}, f32[4,512]{1,0:T(4,128)S(1)}, ...), condition=%wide.region_7.9_spmd, body=%wide.region_4.8_spmd.sunk | while | flops 545258496 | bytes 14042213 | solution.py:22
  99.9 1.9 multiply_reduce_fusion.9
  101.8 1.5 fusion.136
  104.3 1.9 multiply_reduce_fusion.9
  106.2 1.6 fusion.136
  108.7 1.9 multiply_reduce_fusion.9
  110.6 1.5 fusion.136
  113.1 1.9 multiply_reduce_fusion.9
  115.0 1.6 fusion.136
  117.5 1.0 broadcast.120.clone.1
  118.6 16.7 %while.58 = (s32[]{:T(128)}, f32[4,512]{1,0:T(4,128)S(1)}, f32[4,512]{1,0:T(4,128)S(1)}, f32[4,512,128]{2,1,0:T(8,128)}, bf16[4,512,128]{2,1,0:T(8,128)(2,1)}, /...) while((s32[]{:T(128)}, f32[4,512]{1,0:T(4,128)S(1)}, ...), condition=%wide.region_11.13_spmd, body=%wide.region_8.12_spmd.sunk | while | flops 545258496 | bytes 14042213 | solution.py:22
  118.6 1.7 multiply_reduce_fusion.10
  120.2 1.6 fusion.141
  122.7 1.7 multiply_reduce_fusion.10
  124.4 1.6 fusion.141
  126.9 1.7 multiply_reduce_fusion.10
  128.6 1.6 fusion.141
  131.1 1.7 multiply_reduce_fusion.10
  132.8 1.6 fusion.141
  135.4 13.9 %while.59 = (s32[]{:T(128)}, f32[4,512]{1,0:T(4,128)S(1)}, f32[4,512]{1,0:T(4,128)S(1)}, f32[4,512,128]{2,1,0:T(8,128)S(1)}, bf16[4,512,128]{2,1,0:T(8,128)(2,1)...) while((s32[]{:T(128)}, f32[4,512]{1,0:T(4,128)S(1)}, ...), condition=%wide.region_15.17_spmd, body=%wide.region_12.16_spmd.sunk | while | flops 545258496 | bytes 14041705 | solution.py:22
  135.4 1.7 multiply_reduce_fusion.11
  137.1 0.8 fusion.146
  138.0 0.8 fusion.145
  138.9 1.7 multiply_reduce_fusion.11
  140.6 0.9 fusion.146
  141.4 0.8 fusion.145
  142.4 1.7 multiply_reduce_fusion.11
  144.1 0.9 fusion.146
  144.9 0.8 fusion.145
  145.9 1.7 multiply_reduce_fusion.11
  147.6 0.9 fusion.146
  148.4 0.8 fusion.145
  149.4 10.3 %divide_convert_fusion.1 = bf16[2048,1,128]{2,1,0:T(2,128)(2,1)S(1)} fusion(f32[2048,1,128]{2,1,0:T(1,128)} %bitcast.35, f32[2048,1,128]{2,1,0:T(1,128)} %bitcast.34, f32[2048]{0:T(1024)S(1)} %get-tuple-element.230, f32[2048]{0:T(1024)S(1)} %get-tuple-element.232, f32[2048]{0:T(1024)S(1)} %get-tuple-element.231), kind=kLoop, calls=%fused_computation.65 | loop fusion | flops 1310720 | bytes 2646016 | tf_op jit(solution)/shard_map/convert_element_type | solution.py:71
  159.7 10.4 %divide_convert_fusion = bf16[2048,1,128]{2,1,0:T(2,128)(2,1)S(1)} fusion(f32[2048,1,128]{2,1,0:T(1,128)S(1)} %bitcast.223, f32[2048,1,128]{2,1,0:T(1,128)} %bitcast.39, f32[2048]{0:T(1024)S(1)} %get-tuple-element.233, f32[2048]{0:T(1024)S(1)} %get-tuple-element.235, f32[2048]{0:T(1024)S(1)} %get-tuple-element.234), kind=kLoop, calls=%fused_computation.64 | loop fusion | flops 1310720 | bytes 2646016 | tf_op jit(solution)/shard_map/convert_element_type | solution.py:71
  182.7 4.8 %all-to-all-start.3 = ((bf16[16,128,2,128]{3,2,1,0:T(2,128)(2,1)}), bf16[16,128,2,128]{3,2,1,0:T(2,128)(2,1)S(1)}, u32[]{:S(2)}, u32[]{:S(2)}) async-start(bf16[16,128,2,128]{3,2,1,0:T(2,128)(2,1)} %fusion.72), calls=%async_computation.3 | async-start | bytes 2097152 | tf_op jit(solution)/shard_map/all_to_all | solution.py:74
  188.2 24.2 %all-to-all-done.3 = bf16[16,128,2,128]{3,2,1,0:T(2,128)(2,1)S(1)} async-done(((bf16[16,128,2,128]{3,2,1,0:T(2,128)(2,1)}), bf16[16,128,2,128]{3,2,1,0:T(2,128)(2,1)S(1)}, u32[]{:S(2)}, u32[]{:S(2)}) %all-to-all-start.3) | async-done | bytes 1048608 | tf_op jit(solution)/shard_map/all_to_all | solution.py:74
  212.4 0.8 copy.100
  214.0 1.3 copy.101
  (94 shorter events, 25.7 us)
Async XLA Ops:
  0.0 188.1 %copy-start = (f32[35,4096]{1,0:T(8,128)S(1)}, f32[35,4096]{1,0:T(8,128)}, u32[]{:S(2)}) copy-start(f32[35,4096]{1,0:T(8,128)} %param.25) | copy-start | bytes 1720324
  0.0 10.3 %copy-start.4 = (bf16[128,4096]{1,0:T(8,128)(2,1)S(1)}, bf16[128,4096]{1,0:T(8,128)(2,1)}, u32[]{:S(2)}) copy-start(bf16[128,4096]{1,0:T(8,128)(2,1)} %param.19) | copy-start | bytes 3145732
  3.1 31.5 %all-to-all-start = ((bf16[128,32,128]{2,0,1:T(8,128)(2,1)}), bf16[128,32,128]{2,0,1:T(8,128)(2,1)S(1)}, u32[]{:S(2)}, u32[]{:S(2)}) async-start(bf16[128,32,128]{2,0,1:T(8,128)(2,1)} %copy.92), calls=%async_computation | async-start | bytes 2097152 | tf_op jit(solution)/shard_map/all_to_all | solution.py:55
  34.6 9.6 %copy-start.2 = (bf16[128,32,128]{2,0,1:T(8,128)(2,1)}, bf16[128,32,128]{2,0,1:T(8,128)(2,1)S(1)}, u32[]{:S(2)}) copy-start(bf16[128,32,128]{2,0,1:T(8,128)(2,1)S(1)} %all-to-all-done) | copy-start | bytes 3145732
  34.6 29.8 %all-to-all-start.1 = ((bf16[128,32,128]{0,2,1:T(8,128)(2,1)}), bf16[128,32,128]{0,2,1:T(8,128)(2,1)}, u32[]{:S(2)}, u32[]{:S(2)}) async-start(bf16[128,32,128]{0,2,1:T(8,128)(2,1)} %bitcast.22), calls=%async_computation.1 | async-start | bytes 2097152 | tf_op jit(solution)/shard_map/all_to_all | solution.py:56
  44.2 1.2 copy-start.3
  64.4 29.8 %all-to-all-start.2 = ((bf16[128,32,128]{0,2,1:T(8,128)(2,1)}), bf16[128,32,128]{0,2,1:T(8,128)(2,1)}, u32[]{:S(2)}, u32[]{:S(2)}) async-start(bf16[128,32,128]{0,2,1:T(8,128)(2,1)} %bitcast.224), calls=%async_computation.2 | async-start | bytes 2097152 | tf_op jit(solution)/shard_map/all_to_all | solution.py:57
  83.3 13.1 %copy-start.1 = (bf16[4,512,128]{2,1,0:T(8,128)(2,1)}, bf16[4,512,128]{2,1,0:T(8,128)(2,1)S(1)}, u32[]{:S(2)}) copy-start(bf16[4,512,128]{2,1,0:T(8,128)(2,1)S(1)} %get-tuple-element.555) | copy-start | bytes 1572868
  182.7 29.7 %all-to-all-start.3 = ((bf16[16,128,2,128]{3,2,1,0:T(2,128)(2,1)}), bf16[16,128,2,128]{3,2,1,0:T(2,128)(2,1)S(1)}, u32[]{:S(2)}, u32[]{:S(2)}) async-start(bf16[16,128,2,128]{3,2,1,0:T(2,128)(2,1)} %fusion.72), calls=%async_computation.3 | async-start | bytes 2097152 | tf_op jit(solution)/shard_map/all_to_all | solution.py:74
